TPU v7x, 128 devices: a whole 4x4x4 slice. The times are simulated.
128 devices in a mesh: blk: 16 (over z, y), slab: 2 (over x_hi), micro: 4 (over x_lo, core).
Axes of the slice: x: 4 (x_hi: 2, x_lo: 2; x = x_hi * 2 + x_lo), y: 4, z: 4, core: 2. Of those that a mesh axis runs over, the one named last changes fastest.
Arguments:
- displacement: float32 [128, 128, 256], P('blk', 'micro', 'slab'), may hold values from -6 to 6
- load_field: float32 [128, 128, 256], P('blk', 'micro', 'slab'), may hold values from -6 to 6
- foundation: float32 [128, 128, 256], P('blk', 'micro', 'slab'), may hold values from 0.2 to 2
- plastic_flags: int32 [128, 128, 256], P('blk', 'micro', 'slab'), may hold values 0 or 1
- point_slot: int32 [128, 128, 256], P('blk', 'micro', 'slab'), may hold values from 0 to 65535, as said below
- family_in: float32 [4, 3, 256], replicated, may hold values from -5 to 5
- family_mid: bfloat16 [4, 256, 256], replicated, may hold values from -0.375 to 0.375
- family_out: bfloat16 [4, 3, 256], replicated, may hold values from -0.375 to 0.375
- family_tan: float32 [4, 256], replicated, may hold values from 0.002 to 0.02
Outputs:
- updated_field: float32 [128, 128, 256], P('blk', 'micro', 'slab')
- solver_residual: float32 [128, 128, 256], P('blk', 'micro', 'slab')
Inputs may be any that keep to these rules, and one draw needn't show every extreme that they name: `point_slot`: within each device's block of 8 x 32 x 128 nodes the values are distinct; value // 16384 is the point's fibre family and value % 16384 its position among that family's points of the block in node order (last dimension fastest); in every block one family holds exactly 16384 points.
All inputs are finite; a program needn't handle non-finite values. No bound on the sum of `plastic_flags` on one device may be relied on, other than what follows from the above.
Results may differ from a plain program's by a relative error of at most 0.0024.
Values sent between devices are 32-bit elements; how exact they have to be, the bound alone decides.
A program may use at most 128 MiB of HBM per device.

v0:
```python
import jax
import jax.numpy as jnp
from jax import lax
from jax.sharding import PartitionSpec as P

ITERS = 8


def padded_2(cells, sides, width, closed):
    for axis, dim in sides:
        count = lax.axis_size(axis)
        ends = count if closed else count - 1
        head = lax.slice_in_dim(cells, 0, width, axis=dim)
        tail = lax.slice_in_dim(cells, cells.shape[dim] - width, cells.shape[dim], axis=dim)
        cells = jnp.concatenate(
            [
                lax.ppermute(tail, axis, [(i, (i + 1) % count) for i in range(ends)]),
                cells,
                lax.ppermute(head, axis, [((i + 1) % count, i) for i in range(ends)]),
            ],
            axis=dim,
        )
    return cells


def shifted_diff(extended, dim_index, halo_width, margin, length):
    upper_side = lax.slice_in_dim(
        extended, halo_width - margin + 1, halo_width + length + margin + 1, axis=dim_index
    )
    lower_side = lax.slice_in_dim(
        extended, halo_width - margin - 1, halo_width + length + margin - 1, axis=dim_index
    )
    return (upper_side - lower_side) * 0.5


def extend(stacked, halo_width):
    cycle_ext = padded_2(stacked, (("blk", 1),), halo_width, True)
    slab_ext = padded_2(stacked, (("slab", 3), ("micro", 2)), halo_width, False)
    return (cycle_ext, slab_ext)


def gradients(stacked, halo_width, margin):
    size_x, size_y, size_z = stacked.shape[1:]
    cycle_ext, slab_ext = extend(stacked, halo_width)
    along_x = shifted_diff(cycle_ext, 1, halo_width, margin, size_x)
    along_y = shifted_diff(
        lax.slice_in_dim(slab_ext, halo_width, halo_width + size_z, axis=3),
        2,
        halo_width,
        margin,
        size_y,
    )
    along_z = shifted_diff(
        lax.slice_in_dim(slab_ext, halo_width, halo_width + size_y, axis=2),
        3,
        halo_width,
        margin,
        size_z,
    )
    return (along_x, along_y, along_z)


def fibre_model(block_rows, weight_in, weight_mid, weight_out, weight_tan):
    modal = (
        weight_in[0][:, None] * block_rows[0][None, :]
        + weight_in[1][:, None] * block_rows[1][None, :]
        + weight_in[2][:, None] * block_rows[2][None, :]
    )
    active = jnp.where(block_rows[3][None, :] > 0.5, jnp.tanh(modal), modal).astype(jnp.bfloat16)
    hidden = jnp.dot(weight_mid, active, preferred_element_type=jnp.float32)
    bounded = jnp.tanh(hidden).astype(jnp.bfloat16)
    stress = jnp.dot(weight_out, bounded, preferred_element_type=jnp.float32)
    widened = bounded.astype(jnp.float32)
    tangent = 0.5 + jnp.dot(weight_tan, widened * widened, precision=lax.Precision.HIGHEST)
    return jnp.concatenate([stress, tangent[None, :]], axis=0)


def global_sum(value):
    return lax.psum(value, ("blk", "slab", "micro"))


def body(
    displacement,
    load_field,
    foundation,
    plastic_flags,
    point_slot,
    family_in,
    family_mid,
    family_out,
    family_tan,
):
    size_x, size_y, size_z = displacement.shape
    points_dev = size_x * size_y * size_z
    capacity = points_dev // 2
    family_count = family_in.shape[0]
    strain_x, strain_y, strain_z = gradients(displacement[None], 1, 0)
    payload = jnp.concatenate(
        [strain_x, strain_y, strain_z, plastic_flags[None].astype(jnp.float32)], axis=0
    ).reshape(4, points_dev)
    slots = point_slot.reshape(points_dev)
    padded = (
        jnp.zeros((4, family_count * capacity), jnp.float32)
        .at[:, slots]
        .set(payload)
        .reshape(4, family_count, capacity)
    )
    per_family = lax.map(
        lambda inputs: fibre_model(inputs[0], inputs[1], inputs[2], inputs[3], inputs[4]),
        (jnp.moveaxis(padded, 1, 0), family_in, family_mid, family_out, family_tan),
    )
    returned = jnp.moveaxis(per_family, 0, 1)
    answers = returned.reshape(4, family_count * capacity)[:, slots].reshape(
        4, size_x, size_y, size_z
    )
    cycle_ext, slab_ext = extend(answers, 1)
    stress_x = shifted_diff(cycle_ext[0], 0, 1, 0, size_x)
    stress_y = shifted_diff(slab_ext[1][:, :, 1 : 1 + size_z], 1, 1, 0, size_y)
    stress_z = shifted_diff(slab_ext[2][:, 1 : 1 + size_y, :], 2, 1, 0, size_z)
    tangent_x = cycle_ext[3]
    tangent_y = slab_ext[3][:, :, 1 : 1 + size_z]
    tangent_z = slab_ext[3][:, 1 : 1 + size_y, :]
    rhs = load_field - foundation * displacement + (stress_x + stress_y + stress_z)
    solution = jnp.zeros_like(rhs)
    residual = rhs
    direction = rhs
    current = global_sum(jnp.sum(residual * residual))
    for iteration in range(ITERS):
        grad_x, grad_y, grad_z = gradients(direction[None], 2, 1)
        flux_x = tangent_x * grad_x[0]
        flux_y = tangent_y * grad_y[0]
        flux_z = tangent_z * grad_z[0]
        total = (
            shifted_diff(flux_x, 0, 1, 0, size_x)
            + shifted_diff(flux_y, 1, 1, 0, size_y)
            + shifted_diff(flux_z, 2, 1, 0, size_z)
        )
        image = foundation * direction - total
        alpha = current / global_sum(jnp.sum(direction * image))
        solution = solution + alpha * direction
        residual = residual - alpha * image
        following = global_sum(jnp.sum(residual * residual))
        direction = residual + following / current * direction
        current = following
    return (displacement + solution, residual)


def solution(mesh):
    placed = (
        P("blk", "micro", "slab"),
        P("blk", "micro", "slab"),
        P("blk", "micro", "slab"),
        P("blk", "micro", "slab"),
        P("blk", "micro", "slab"),
        P(),
        P(),
        P(),
        P(),
    )
    return jax.shard_map(
        body,
        mesh=mesh,
        in_specs=placed,
        out_specs=(P("blk", "micro", "slab"), P("blk", "micro", "slab")),
        check_vma=False,
    )
```

profile of v0, /device:TPU:1, one launch (start us, length us, event | category | flops | bytes accessed | tf_op | source)
XLA Modules:
  0.0 1535.5 jit_solution(5746683782115413864)
XLA Ops:
  1.7 5.5 collective-permute-start.2
  9.2 6.2 collective-permute-start
  27.0 8.4 copy.40
  35.4 93.5 %scatter_custom_fusion = f32[4,65536]{0,1:T(8,128)} fusion(s32[32768]{0:T(1024)S(1)} %bitcast.213, f32[32768,4]{1,0:T(8,128)} %copy.40, f32[]{:T(128)} %constant.13.clone.1), kind=kCustom, calls=%fused_computation.34 | custom fusion | bytes 1049088 | tf_op jit(solution)/shard_map/scatter | solution.py:105
  128.8 18.1 %copy.41 = f32[4,4,16384]{2,0,1:T(4,128)S(1)} copy(f32[4,4,16384]{0,2,1:T(8,128)} %bitcast.150) | data formatting | bytes 2097152 | tf_op jit(solution)/shard_map/reshape | solution.py:106
  146.9 78.6 %while.10 = (s32[]{:T(128)}, f32[4,4,16384]{2,1,0:T(4,128)S(1)}, bf16[4,3,256]{2,1,0:T(4,128)(2,1)S(1)}, bf16[4,256,256]{2,1,0:T(8,128)(2,1)}, f32[4,4,16384]{2,...) while((s32[]{:T(128)}, f32[4,4,16384]{2,1,0:T(4,128)S(1)}, ...), condition=%wide.region_2.3_spmd, body=%wide.region_1.2_spmd.sunk | while | flops 2265022464 | bytes 26981568 | solution.py:108
  148.2 7.5 fusion.180
  156.9 9.5 fusion.181
  167.7 7.5 fusion.180
  176.4 9.5 fusion.181
  187.2 7.5 fusion.180
  195.9 9.5 fusion.181
  206.7 7.5 fusion.180
  215.4 9.5 fusion.181
  225.5 16.1 %copy.43 = f32[4,4,16384]{0,2,1:T(8,128)} copy(f32[4,4,16384]{2,0,1:T(4,128)S(1)} %bitcast.211) | data formatting | bytes 2097152 | tf_op jit(solution)/shard_map/transpose | solution.py:112
  241.5 119.1 %gather_fusion = f32[32768,4]{1,0:T(8,128)} fusion(f32[4,65536]{0,1:T(8,128)} %bitcast.151, s32[32768]{0:T(1024)S(1)} %broadcast_clamp_fusion), kind=kCustom, calls=%fused_computation | custom fusion | bytes 1179648 | tf_op jit(solution)/shard_map/gather | solution.py:113
  360.6 10.0 copy.45
  370.8 6.1 collective-permute-start.8
  378.3 10.2 collective-permute-done.8
  388.5 5.4 collective-permute-done.9
  398.5 5.1 collective-permute-start.6
  405.5 5.5 collective-permute-done.7
  415.4 4.9 collective-permute-done.15
  428.5 61.8 %all-reduce = (f32[]{:T(128)}, f32[]{:T(128)}) all-reduce(f32[]{:T(128)} %get-tuple-element.55, f32[]{:T(128)} %get-tuple-element.54), channel_id=1, replica_groups=mesh['blk'=16,'slab'=2,'micro'=4] {'blk','slab','micro'}, use_global_device_ids=true, to_apply=%region_4.5 | all-reduce | flops 2 | bytes 16 | tf_op jit(solution)/shard_map/psum | solution.py:79
  492.3 64.1 %psum.114 = f32[]{:T(128)} all-reduce(f32[]{:T(128)} %multiply_reduce_fusion.13), channel_id=1, replica_groups=mesh['blk'=16,'slab'=2,'micro'=4] {'blk','slab','micro'}, use_global_device_ids=true, to_apply=%region_8.9 | all-reduce | flops 1 | bytes 8 | tf_op jit(solution)/shard_map/psum | solution.py:79
  564.3 4.4 collective-permute-done.21
  568.8 4.3 collective-permute-start.22
  577.2 62.9 %psum.115 = f32[]{:T(128)} all-reduce(f32[]{:T(128)} %get-tuple-element.96), channel_id=1, replica_groups=mesh['blk'=16,'slab'=2,'micro'=4] {'blk','slab','micro'}, use_global_device_ids=true, to_apply=%region_10.11 | all-reduce | flops 1 | bytes 8 | tf_op jit(solution)/shard_map/psum | solution.py:79
  642.1 62.6 %psum.116 = f32[]{:T(128)} all-reduce(f32[]{:T(128)} %get-tuple-element.94), channel_id=1, replica_groups=mesh['blk'=16,'slab'=2,'micro'=4] {'blk','slab','micro'}, use_global_device_ids=true, to_apply=%region_12.13 | all-reduce | flops 1 | bytes 8 | tf_op jit(solution)/shard_map/psum | solution.py:79
  712.8 4.5 collective-permute-done.27
  725.8 62.5 %psum.117 = f32[]{:T(128)} all-reduce(f32[]{:T(128)} %get-tuple-element.92), channel_id=1, replica_groups=mesh['blk'=16,'slab'=2,'micro'=4] {'blk','slab','micro'}, use_global_device_ids=true, to_apply=%region_14.15 | all-reduce | flops 1 | bytes 8 | tf_op jit(solution)/shard_map/psum | solution.py:79
  790.3 63.9 %psum.118 = f32[]{:T(128)} all-reduce(f32[]{:T(128)} %get-tuple-element.90), channel_id=1, replica_groups=mesh['blk'=16,'slab'=2,'micro'=4] {'blk','slab','micro'}, use_global_device_ids=true, to_apply=%region_16.17 | all-reduce | flops 1 | bytes 8 | tf_op jit(solution)/shard_map/psum | solution.py:79
  861.8 4.3 collective-permute-done.33
  866.2 4.3 collective-permute-start.34
  874.6 63.2 %psum.119 = f32[]{:T(128)} all-reduce(f32[]{:T(128)} %get-tuple-element.88), channel_id=1, replica_groups=mesh['blk'=16,'slab'=2,'micro'=4] {'blk','slab','micro'}, use_global_device_ids=true, to_apply=%region_18.19 | all-reduce | flops 1 | bytes 8 | tf_op jit(solution)/shard_map/psum | solution.py:79
  939.8 62.6 %psum.120 = f32[]{:T(128)} all-reduce(f32[]{:T(128)} %get-tuple-element.86), channel_id=1, replica_groups=mesh['blk'=16,'slab'=2,'micro'=4] {'blk','slab','micro'}, use_global_device_ids=true, to_apply=%region_20.21 | all-reduce | flops 1 | bytes 8 | tf_op jit(solution)/shard_map/psum | solution.py:79
  1010.2 4.5 collective-permute-done.39
  1023.7 62.4 %psum.121 = f32[]{:T(128)} all-reduce(f32[]{:T(128)} %get-tuple-element.84), channel_id=1, replica_groups=mesh['blk'=16,'slab'=2,'micro'=4] {'blk','slab','micro'}, use_global_device_ids=true, to_apply=%region_22.23 | all-reduce | flops 1 | bytes 8 | tf_op jit(solution)/shard_map/psum | solution.py:79
  1088.2 63.6 %psum.122 = f32[]{:T(128)} all-reduce(f32[]{:T(128)} %get-tuple-element.82), channel_id=1, replica_groups=mesh['blk'=16,'slab'=2,'micro'=4] {'blk','slab','micro'}, use_global_device_ids=true, to_apply=%region_24.25 | all-reduce | flops 1 | bytes 8 | tf_op jit(solution)/shard_map/psum | solution.py:79
  1163.9 4.2 collective-permute-start.46
  1172.2 63.2 %psum.123 = f32[]{:T(128)} all-reduce(f32[]{:T(128)} %get-tuple-element.80), channel_id=1, replica_groups=mesh['blk'=16,'slab'=2,'micro'=4] {'blk','slab','micro'}, use_global_device_ids=true, to_apply=%region_26.27 | all-reduce | flops 1 | bytes 8 | tf_op jit(solution)/shard_map/psum | solution.py:79
  1237.4 62.6 %psum.124 = f32[]{:T(128)} all-reduce(f32[]{:T(128)} %get-tuple-element.78), channel_id=1, replica_groups=mesh['blk'=16,'slab'=2,'micro'=4] {'blk','slab','micro'}, use_global_device_ids=true, to_apply=%region_28.29 | all-reduce | flops 1 | bytes 8 | tf_op jit(solution)/shard_map/psum | solution.py:79
  1307.9 4.4 collective-permute-done.51
  1321.2 62.7 %psum.125 = f32[]{:T(128)} all-reduce(f32[]{:T(128)} %get-tuple-element.76), channel_id=1, replica_groups=mesh['blk'=16,'slab'=2,'micro'=4] {'blk','slab','micro'}, use_global_device_ids=true, to_apply=%region_30.31 | all-reduce | flops 1 | bytes 8 | tf_op jit(solution)/shard_map/psum | solution.py:79
  1385.8 63.5 %psum.126 = f32[]{:T(128)} all-reduce(f32[]{:T(128)} %get-tuple-element.74), channel_id=1, replica_groups=mesh['blk'=16,'slab'=2,'micro'=4] {'blk','slab','micro'}, use_global_device_ids=true, to_apply=%region_32.33 | all-reduce | flops 1 | bytes 8 | tf_op jit(solution)/shard_map/psum | solution.py:79
  1457.1 4.4 collective-permute-done.57
  1461.6 4.2 collective-permute-start.58
  1469.9 63.2 %psum.127 = f32[]{:T(128)} all-reduce(f32[]{:T(128)} %get-tuple-element.72), channel_id=1, replica_groups=mesh['blk'=16,'slab'=2,'micro'=4] {'blk','slab','micro'}, use_global_device_ids=true, to_apply=%region_34.35 | all-reduce | flops 1 | bytes 8 | tf_op jit(solution)/shard_map/psum | solution.py:79
  (218 shorter events, 142.7 us)
Async XLA Ops:
  1.7 14.8 collective-permute-start.2
  7.2 9.3 collective-permute-start.3
  9.2 15.4 %collective-permute-start = (f32[1,1,32,128]{3,2,1,0:T(8,128)S(1)}, f32[1,1,32,128]{3,2,1,0:T(8,128)S(1)}, u32[]{:S(2)}, u32[]{:S(2)}) collective-permute-start(f32[1,1,32,128]{3,2,1,0:T(8,128)S(1)} %get-tuple-element.169), channel_id=1, source_target_pairs={{8,0},{16,8},{24,16},{32,24},{40,32},{48,40},{56,48},{64,56},{72,6... | collective-permute-start | bytes 49160 | tf_op jit(solution)/shard_map/ppermute | solution.py:19
  15.4 9.2 collective-permute-start.1
  17.4 7.2 collective-permute-start.4
  370.8 17.7 %collective-permute-start.8 = (f32[4,8,32,1]{3,2,1,0:T(8,128)S(1)}, f32[4,8,32,1]{3,2,1,0:T(8,128)S(1)}, u32[]{:S(2)}, u32[]{:S(2)}) collective-permute-start(f32[4,8,32,1]{3,2,1,0:T(8,128)S(1)} %get-tuple-element.114), channel_id=1, source_target_pairs={{0,4},{1,5},{2,6},{3,7},{8,12},{9,13},{10,14},{11,15},{16,20},{17,... | collective-permute-start | bytes 12296 | tf_op jit(solution)/shard_map/ppermute | solution.py:17
  377.0 16.9 %collective-permute-start.9 = (f32[4,8,32,1]{3,2,1,0:T(8,128)S(1)}, f32[4,8,32,1]{3,2,1,0:T(8,128)S(1)}, u32[]{:S(2)}, u32[]{:S(2)}) collective-permute-start(f32[4,8,32,1]{3,2,1,0:T(8,128)S(1)} %get-tuple-element.115), channel_id=1, source_target_pairs={{4,0},{5,1},{6,2},{7,3},{12,8},{13,9},{14,10},{15,11},{20,16},{21,... | collective-permute-start | bytes 12296 | tf_op jit(solution)/shard_map/ppermute | solution.py:19
  394.1 9.5 collective-permute-start.10
  396.1 7.6 collective-permute-start.11
  398.5 7.0 collective-permute-start.6
  403.6 7.3 collective-permute-start.7
  412.5 7.8 collective-permute-start.15
  413.8 13.9 collective-permute-start.12
  413.9 13.8 collective-permute-start.13
  420.4 6.4 collective-permute-start.16
  557.8 6.5 collective-permute-start.20
  561.4 7.2 collective-permute-start.21
  562.7 13.7 collective-permute-start.18
  564.0 12.4 collective-permute-start.19
  568.8 6.4 collective-permute-start.22
  706.1 6.7 collective-permute-start.26
  709.8 7.5 collective-permute-start.27
  711.1 14.0 collective-permute-start.24
  712.4 12.6 collective-permute-start.25
  717.4 6.7 collective-permute-start.28
  858.8 7.2 collective-permute-start.33
  860.2 13.7 collective-permute-start.30
  861.8 12.0 collective-permute-start.31
  866.2 6.4 collective-permute-start.34
  1003.8 6.4 collective-permute-start.38
  1007.2 7.5 collective-permute-start.39
  1008.5 14.5 collective-permute-start.36
  1010.2 12.8 collective-permute-start.37
  1014.8 7.2 collective-permute-start.40
  1153.2 6.4 collective-permute-start.44
  1156.6 7.2 collective-permute-start.45
  1157.9 13.5 collective-permute-start.42
  1159.4 12.0 collective-permute-start.43
  1163.9 6.3 collective-permute-start.46
  1301.4 6.5 collective-permute-start.50
  1304.7 7.5 collective-permute-start.51
  1306.0 14.3 collective-permute-start.48
  1307.9 12.5 collective-permute-start.49
  1312.4 7.1 collective-permute-start.52
  1454.3 7.2 collective-permute-start.57
  1455.6 13.5 collective-permute-start.54
  1457.1 12.0 collective-permute-start.55
  1461.6 6.3 collective-permute-start.58
  (15 other events, 556.9 us)
where the time goes:
time: 1550 us; the launch traced here: 1540 us
  blocking collectives  945 us (61%)
  local copies, waits for them, and re-layouts  272 us (18%)
  starting transfers between devices  136 us (9%)
  matrix products  72.6 us (5%)
  waiting for transfers between devices  64.8 us (4%)
  other arithmetic  22.7 us (1%)
  between operations  22 us (1%)
    psum x15, blocking collectives, global_sum(): return lax.psum(value, ('blk', 'slab', 'micro'))  945 us
    gather x1, local copies, waits for them, and re-layouts, body(): returned.reshape(4, family_count * capacity)[:, slots]  119 us
    scatter x1, local copies, waits for them, and re-layouts, body(): padded = jnp.zeros((4, family_count * capacity), jnp.float32).at[:, slots...  93.5 us
    ppermute x30, starting transfers between devices, padded_2(): lax.ppermute(head, axis, [((i + 1) % count, i) for i in range(ends)])  72.3 us
    ppermute x30, starting transfers between devices, padded_2(): lax.ppermute(tail, axis, [(i, (i + 1) % count) for i in range(ends)])  63.5 us
    ppermute x30, waiting for transfers between devices, padded_2(): lax.ppermute(head, axis, [((i + 1) % count, i) for i in range(ends)])  42.2 us
    dot_general x4, matrix products, fibre_model(): jnp.dot(weight_tan, widened * widened, precision=lax.Precision.HIGHEST)  37.9 us
  transfers between devices with their start and end apart: 60, of which 20 were waited for; matrix products, arithmetic and copies ran while one was open for 1% of the time, Pallas kernels for 0%

commit v1 on v0

--- a/solution.py
+++ b/solution.py
@@ -76,7 +76,11 @@
 
 
 def global_sum(value):
-    return lax.psum(value, ("blk", "slab", "micro"))
+
+    def record_link(local_array):
+        return lax.all_gather(local_array, ("blk", "slab", "micro")).sum(axis=0)
+
+    return record_link(value)
 
 
 def body(

time: 1550 us -> 1570 us (1.013)
    psum x15 -> x0, blocking collectives: 945 us -> none  [global_sum(): return lax.psum(value, ('blk', 'slab', 'micro'))]
    unnamed x0 -> x15, blocking collectives: none -> 943 us
where the time goes in v1:
time: 1570 us; the launch traced here: 1560 us
  blocking collectives  943 us (60%)
  local copies, waits for them, and re-layouts  285 us (18%)
  starting transfers between devices  136 us (9%)
  matrix products  72.6 us (5%)
  waiting for transfers between devices  65 us (4%)
  other arithmetic  32.2 us (2%)
  between operations  22 us (1%)
    unnamed x15, blocking collectives  943 us
    gather x1, local copies, waits for them, and re-layouts, body(): returned.reshape(4, family_count * capacity)[:, slots]  119 us
    scatter x1, local copies, waits for them, and re-layouts, body(): padded = jnp.zeros((4, family_count * capacity), jnp.float32).at[:, slots...  93.5 us
    ppermute x30, starting transfers between devices, padded_2(): lax.ppermute(head, axis, [((i + 1) % count, i) for i in range(ends)])  72.4 us
    ppermute x30, starting transfers between devices, padded_2(): lax.ppermute(tail, axis, [(i, (i + 1) % count) for i in range(ends)])  63.5 us
    ppermute x30, waiting for transfers between devices, padded_2(): lax.ppermute(head, axis, [((i + 1) % count, i) for i in range(ends)])  42.2 us
    dot_general x4, matrix products, fibre_model(): jnp.dot(weight_tan, widened * widened, precision=lax.Precision.HIGHEST)  37.9 us
  transfers between devices with their start and end apart: 60, of which 20 were waited for; matrix products, arithmetic and copies ran while one was open for 1% of the time, Pallas kernels for 0%

profile of v1, /device:TPU:1, one launch (start us, length us, event | category | flops | bytes accessed | tf_op | source)
XLA Modules:
  0.0 1556.7 jit_solution(3632382578997144311)
XLA Ops:
  1.7 5.5 collective-permute-start.2
  9.2 6.2 collective-permute-start
  27.0 8.5 copy.40
  35.4 93.5 %scatter_custom_fusion = f32[4,65536]{0,1:T(8,128)} fusion(s32[32768]{0:T(1024)S(1)} %bitcast.229, f32[32768,4]{1,0:T(8,128)} %copy.40, f32[]{:T(128)} %constant.13.clone.1), kind=kCustom, calls=%fused_computation.34 | custom fusion | bytes 1049088 | tf_op jit(solution)/shard_map/scatter | solution.py:109
  128.9 18.1 %copy.41 = f32[4,4,16384]{2,0,1:T(4,128)S(1)} copy(f32[4,4,16384]{0,2,1:T(8,128)} %bitcast.166) | data formatting | bytes 2097152 | tf_op jit(solution)/shard_map/reshape | solution.py:110
  147.0 78.4 %while.10 = (s32[]{:T(128)}, f32[4,4,16384]{2,1,0:T(4,128)S(1)}, bf16[4,3,256]{2,1,0:T(4,128)(2,1)S(1)}, bf16[4,256,256]{2,1,0:T(8,128)(2,1)}, f32[4,4,16384]{2,...) while((s32[]{:T(128)}, f32[4,4,16384]{2,1,0:T(4,128)S(1)}, ...), condition=%wide.region_2.3_spmd, body=%wide.region_1.2_spmd.sunk | while | flops 2265022464 | bytes 26981568 | solution.py:112
  148.3 7.5 fusion.180
  157.0 9.5 fusion.181
  167.8 7.5 fusion.180
  176.5 9.5 fusion.181
  187.3 7.5 fusion.180
  196.0 9.5 fusion.181
  206.8 7.5 fusion.180
  215.5 9.5 fusion.181
  225.4 16.1 %copy.43 = f32[4,4,16384]{0,2,1:T(8,128)} copy(f32[4,4,16384]{2,0,1:T(4,128)S(1)} %bitcast.227) | data formatting | bytes 2097152 | tf_op jit(solution)/shard_map/transpose | solution.py:116
  241.5 118.9 %gather_fusion = f32[32768,4]{1,0:T(8,128)} fusion(f32[4,65536]{0,1:T(8,128)} %bitcast.167, s32[32768]{0:T(1024)S(1)} %broadcast_clamp_fusion), kind=kCustom, calls=%fused_computation | custom fusion | bytes 1179648 | tf_op jit(solution)/shard_map/gather | solution.py:117
  360.4 10.0 copy.45
  371.4 6.1 collective-permute-start.8
  378.8 10.6 collective-permute-done.8
  389.3 5.1 collective-permute-done.9
  399.0 5.1 collective-permute-start.6
  406.0 5.5 collective-permute-done.7
  415.9 4.9 collective-permute-done.15
  430.6 61.7 %all-reduce.16 = (f32[128]{0:T(128)S(1)}, f32[128]{0:T(128)S(1)}) all-reduce(f32[128]{0:T(128)S(1)} %dynamic-update-slice, f32[128]{0:T(128)S(1)} %dynamic-update-slice.1), channel_id=1, replica_groups=mesh['blk'=16,'slab'=2,'micro'=4] {'blk','slab','micro'}, use_global_device_ids=true, to_apply=%add | all-reduce | flops 256 | bytes 2048
  496.2 64.0 %all-reduce.2 = f32[128]{0:T(128)S(1)} all-reduce(f32[128]{0:T(128)S(1)} %dynamic-update-slice.2), channel_id=1, replica_groups=mesh['blk'=16,'slab'=2,'micro'=4] {'blk','slab','micro'}, use_global_device_ids=true, to_apply=%add.2 | all-reduce | flops 128 | bytes 1024
  568.7 4.4 collective-permute-done.21
  573.2 4.4 collective-permute-start.22
  582.5 62.4 %all-reduce.3 = f32[128]{0:T(128)S(1)} all-reduce(f32[128]{0:T(128)S(1)} %dynamic-update-slice.3), channel_id=1, replica_groups=mesh['blk'=16,'slab'=2,'micro'=4] {'blk','slab','micro'}, use_global_device_ids=true, to_apply=%add.3 | all-reduce | flops 128 | bytes 1024
  648.3 63.5 %all-reduce.4 = f32[128]{0:T(128)S(1)} all-reduce(f32[128]{0:T(128)S(1)} %dynamic-update-slice.4), channel_id=1, replica_groups=mesh['blk'=16,'slab'=2,'micro'=4] {'blk','slab','micro'}, use_global_device_ids=true, to_apply=%add.4 | all-reduce | flops 128 | bytes 1024
  720.3 4.4 collective-permute-done.27
  724.8 4.2 collective-permute-start.28
  733.8 63.0 %all-reduce.5 = f32[128]{0:T(128)S(1)} all-reduce(f32[128]{0:T(128)S(1)} %dynamic-update-slice.5), channel_id=1, replica_groups=mesh['blk'=16,'slab'=2,'micro'=4] {'blk','slab','micro'}, use_global_device_ids=true, to_apply=%add.5 | all-reduce | flops 128 | bytes 1024
  800.2 62.6 %all-reduce.6 = f32[128]{0:T(128)S(1)} all-reduce(f32[128]{0:T(128)S(1)} %dynamic-update-slice.6), channel_id=1, replica_groups=mesh['blk'=16,'slab'=2,'micro'=4] {'blk','slab','micro'}, use_global_device_ids=true, to_apply=%add.6 | all-reduce | flops 128 | bytes 1024
  871.1 4.5 collective-permute-done.33
  885.3 62.4 %all-reduce.7 = f32[128]{0:T(128)S(1)} all-reduce(f32[128]{0:T(128)S(1)} %dynamic-update-slice.7), channel_id=1, replica_groups=mesh['blk'=16,'slab'=2,'micro'=4] {'blk','slab','micro'}, use_global_device_ids=true, to_apply=%add.7 | all-reduce | flops 128 | bytes 1024
  951.0 63.7 %all-reduce.8 = f32[128]{0:T(128)S(1)} all-reduce(f32[128]{0:T(128)S(1)} %dynamic-update-slice.8), channel_id=1, replica_groups=mesh['blk'=16,'slab'=2,'micro'=4] {'blk','slab','micro'}, use_global_device_ids=true, to_apply=%add.8 | all-reduce | flops 128 | bytes 1024
  1023.1 4.3 collective-permute-done.39
  1027.5 4.3 collective-permute-start.40
  1036.6 63.3 %all-reduce.9 = f32[128]{0:T(128)S(1)} all-reduce(f32[128]{0:T(128)S(1)} %dynamic-update-slice.9), channel_id=1, replica_groups=mesh['blk'=16,'slab'=2,'micro'=4] {'blk','slab','micro'}, use_global_device_ids=true, to_apply=%add.9 | all-reduce | flops 128 | bytes 1024
  1103.3 62.6 %all-reduce.10 = f32[128]{0:T(128)S(1)} all-reduce(f32[128]{0:T(128)S(1)} %dynamic-update-slice.10), channel_id=1, replica_groups=mesh['blk'=16,'slab'=2,'micro'=4] {'blk','slab','micro'}, use_global_device_ids=true, to_apply=%add.10 | all-reduce | flops 128 | bytes 1024
  1174.3 4.5 collective-permute-done.45
  1188.5 62.4 %all-reduce.11 = f32[128]{0:T(128)S(1)} all-reduce(f32[128]{0:T(128)S(1)} %dynamic-update-slice.11), channel_id=1, replica_groups=mesh['blk'=16,'slab'=2,'micro'=4] {'blk','slab','micro'}, use_global_device_ids=true, to_apply=%add.11 | all-reduce | flops 128 | bytes 1024
  1254.3 63.5 %all-reduce.12 = f32[128]{0:T(128)S(1)} all-reduce(f32[128]{0:T(128)S(1)} %dynamic-update-slice.12), channel_id=1, replica_groups=mesh['blk'=16,'slab'=2,'micro'=4] {'blk','slab','micro'}, use_global_device_ids=true, to_apply=%add.12 | all-reduce | flops 128 | bytes 1024
  1326.1 4.4 collective-permute-done.51
  1339.6 63.2 %all-reduce.13 = f32[128]{0:T(128)S(1)} all-reduce(f32[128]{0:T(128)S(1)} %dynamic-update-slice.13), channel_id=1, replica_groups=mesh['blk'=16,'slab'=2,'micro'=4] {'blk','slab','micro'}, use_global_device_ids=true, to_apply=%add.13 | all-reduce | flops 128 | bytes 1024
  1406.1 62.6 %all-reduce.14 = f32[128]{0:T(128)S(1)} all-reduce(f32[128]{0:T(128)S(1)} %dynamic-update-slice.14), channel_id=1, replica_groups=mesh['blk'=16,'slab'=2,'micro'=4] {'blk','slab','micro'}, use_global_device_ids=true, to_apply=%add.14 | all-reduce | flops 128 | bytes 1024
  1477.1 4.4 collective-permute-done.57
  1491.4 62.4 %all-reduce.15 = f32[128]{0:T(128)S(1)} all-reduce(f32[128]{0:T(128)S(1)} %dynamic-update-slice.15), channel_id=1, replica_groups=mesh['blk'=16,'slab'=2,'micro'=4] {'blk','slab','micro'}, use_global_device_ids=true, to_apply=%add.15 | all-reduce | flops 128 | bytes 1024
  (266 shorter events, 165.4 us)
Async XLA Ops:
  1.7 14.8 collective-permute-start.2
  7.2 9.3 collective-permute-start.3
  9.2 15.4 collective-permute-start
  15.4 9.2 collective-permute-start.1
  17.4 7.2 collective-permute-start.4
  371.4 18.0 %collective-permute-start.8 = (f32[4,8,32,1]{3,2,1,0:T(8,128)}, f32[4,8,32,1]{3,2,1,0:T(8,128)S(1)}, u32[]{:S(2)}, u32[]{:S(2)}) collective-permute-start(f32[4,8,32,1]{3,2,1,0:T(8,128)} %get-tuple-element.114), channel_id=1, source_target_pairs={{0,4},{1,5},{2,6},{3,7},{8,12},{9,13},{10,14},{11,15},{16,20},{17,... | collective-permute-start | bytes 12296 | tf_op jit(solution)/shard_map/ppermute | solution.py:17
  377.5 16.9 %collective-permute-start.9 = (f32[4,8,32,1]{3,2,1,0:T(8,128)S(1)}, f32[4,8,32,1]{3,2,1,0:T(8,128)S(1)}, u32[]{:S(2)}, u32[]{:S(2)}) collective-permute-start(f32[4,8,32,1]{3,2,1,0:T(8,128)S(1)} %get-tuple-element.115), channel_id=1, source_target_pairs={{4,0},{5,1},{6,2},{7,3},{12,8},{13,9},{14,10},{15,11},{20,16},{21,... | collective-permute-start | bytes 12296 | tf_op jit(solution)/shard_map/ppermute | solution.py:19
  394.7 9.5 collective-permute-start.10
  396.6 7.6 collective-permute-start.11
  399.0 7.0 collective-permute-start.6
  404.2 7.3 collective-permute-start.7
  413.1 7.8 collective-permute-start.15
  414.4 13.9 collective-permute-start.12
  414.5 13.8 collective-permute-start.13
  421.0 6.4 collective-permute-start.16
  562.2 6.5 collective-permute-start.20
  565.9 7.2 collective-permute-start.21
  567.2 13.8 collective-permute-start.18
  568.5 12.5 collective-permute-start.19
  573.2 6.5 collective-permute-start.22
  713.9 6.4 collective-permute-start.26
  717.4 7.2 collective-permute-start.27
  718.8 13.5 collective-permute-start.24
  720.1 12.2 collective-permute-start.25
  864.8 6.4 collective-permute-start.32
  868.1 7.5 collective-permute-start.33
  869.4 14.3 collective-permute-start.30
  871.1 12.6 collective-permute-start.31
  875.8 7.1 collective-permute-start.34
  1020.1 7.2 collective-permute-start.39
  1021.4 13.7 collective-permute-start.36
  1023.1 12.1 collective-permute-start.37
  1027.5 6.4 collective-permute-start.40
  1167.9 6.4 collective-permute-start.44
  1171.2 7.5 collective-permute-start.45
  1172.6 14.5 collective-permute-start.42
  1174.3 12.8 collective-permute-start.43
  1178.9 7.2 collective-permute-start.46
  1319.8 6.3 collective-permute-start.50
  1323.2 7.2 collective-permute-start.51
  1324.6 13.5 collective-permute-start.48
  1326.0 12.0 collective-permute-start.49
  1330.6 6.3 collective-permute-start.52
  1470.7 6.4 collective-permute-start.56
  1474.0 7.5 collective-permute-start.57
  1475.3 14.5 collective-permute-start.54
  1477.1 12.8 collective-permute-start.55
  1481.7 7.3 collective-permute-start.58
  (15 other events, 559.2 us)
